TPU v7x, 256 devices: a whole 4x4x8 slice. The times are simulated.
256 devices in a mesh: seq: 32 (over y, z), tensor: 8 (over x, core).
Axes of the slice: x: 4, y: 4, z: 8, core: 2. Of those that a mesh axis runs over, the one named last changes fastest.
Arguments:
- state: bfloat16 [32768, 2048], P('seq', 'tensor'), may hold values from -20.5 to 20.5
- memory: bfloat16 [512, 2048], P('seq', 'tensor'), may hold values from -20.5 to 20.5
- w_query: bfloat16 [2048, 2048], P('seq', 'tensor'), may hold values from -0.1875 to 0.1875
- w_key: bfloat16 [2048, 2048], P('seq', 'tensor'), may hold values from -0.1875 to 0.1875
- w_value: bfloat16 [2048, 2048], P('seq', 'tensor'), may hold values from -0.125 to 0.125
- w_output: bfloat16 [2048, 2048], P('tensor', 'seq'), may hold values from -0.375 to 0.375
- norm_gain: float32 [2048], P('tensor'), may hold values from 0.1 to 1.9
- remaining: int32 [32768], P('seq'), may hold values from 0 to 3
- slot_home: int32 [512], replicated, may hold values from 0 to 31
Outputs:
- new_state: bfloat16 [32768, 2048], P('seq', 'tensor')
- new_memory: bfloat16 [512, 2048], P('seq', 'tensor')
Inputs may be any that keep to these rules, and one draw needn't show every extreme that they name: `remaining`: 0 means the token has halted.
All inputs are finite; a program needn't handle non-finite values.
Results may differ from a plain program's by a relative error of at most 0.014.
The roundings to bfloat16 on the way count: a program that leaves them out, or rounds other values in their place, can miss the bound.
Values may be sent and summed in bfloat16 or wider, within the bound.
No kernel may reach another device: no remote copies, remote signals or barrier semaphores. Data moves between devices by JAX's collectives and lax.ppermute only.
A program may use at most 128 MiB of HBM per device.

v0:
```python
import math
import jax
import jax.numpy as jnp
from jax import lax
from jax.sharding import PartitionSpec as P

D = 2048
H = 16
HD = 128
HALF = 256
QB = 512
EPS = 1e-05
MASKED = -1e30


def with_halo(array, sides, width):
    for axis, dim in sides:
        peers, length = (lax.axis_size(axis), array.shape[dim])
        up = [(i, (i + 1) % peers) for i in range(peers - 1)]
        down = [(j, i) for i, j in up]
        last = lax.slice_in_dim(array, length - width, length, axis=dim)
        initial = lax.slice_in_dim(array, 0, width, axis=dim)
        before = lax.ppermute(last, axis, up)
        after = lax.ppermute(initial, axis, down)
        array = jnp.concatenate([before, array, after], axis=dim)
    return array


def merged(part, axis, combine):
    gathered = jax.tree.map(lambda a: lax.all_gather(a, axis), part)

    def take(source):
        return jax.tree.map(lambda a: lax.dynamic_index_in_dim(a, source, 0, False), gathered)

    return lax.fori_loop(
        1, lax.axis_size(axis), lambda source, state: combine(state, take(source)), take(0)
    )


def head_slopes(first, amount):
    order = (first + jnp.arange(amount, dtype=jnp.int32)).astype(jnp.float32)
    return 0.25 * 8.0 ** (order / (H - 1))


def shards(state, memory, w_query, w_key, w_value, w_output, norm_gain, remaining, slot_home):
    tok_rows = state.shape[0]
    slot_rows = memory.shape[0]
    seq_count = lax.axis_size("seq")
    seq_place = lax.axis_index("seq")
    tensor_place = lax.axis_index("tensor")
    local_width = w_query.shape[1]
    local_heads = local_width // HD
    total_tokens = tok_rows * seq_count
    score_scale = 1.0 / math.sqrt(HD)
    distance_slopes = head_slopes(tensor_place * local_heads, local_heads)
    homes = slot_home.astype(jnp.float32)
    home_gap = jnp.abs(homes - seq_place.astype(jnp.float32))
    slot_bias = distance_slopes[:, None] * home_gap[None, :]
    state_full, memory_full = (
        lax.all_gather(state, "tensor", axis=1, tiled=True),
        lax.all_gather(memory, "tensor", axis=1, tiled=True),
    )
    rows_full = jnp.concatenate([state_full, memory_full], axis=0)
    pieces = (
        lax.all_gather(w_query, "seq", axis=0, tiled=True),
        lax.all_gather(w_key, "seq", axis=0, tiled=True),
        lax.all_gather(w_value, "seq", axis=0, tiled=True),
    )
    query_acc, key_acc, value_acc = tuple(
        (jnp.dot(rows_full, piece, preferred_element_type=jnp.float32) for piece in pieces)
    )
    query = query_acc.astype(jnp.bfloat16)
    keys = key_acc.astype(jnp.bfloat16)
    values = value_acc.astype(jnp.bfloat16)
    slot_heads = jnp.concatenate([query[tok_rows:], keys[tok_rows:], values[tok_rows:]], axis=1)
    all_slots = lax.all_gather(slot_heads, "seq", axis=0, tiled=True)
    memory_slot_query = all_slots[:, :local_width].reshape(-1, local_heads, HD)
    memory_slot_keys = all_slots[:, local_width : 2 * local_width].reshape(-1, local_heads, HD)
    memory_slot_values = all_slots[:, 2 * local_width :].reshape(-1, local_heads, HD)
    token_key_rows = keys[:tok_rows].reshape(tok_rows, local_heads, HD)
    token_value_rows = values[:tok_rows].reshape(tok_rows, local_heads, HD)
    keys_values = jnp.concatenate([keys[:tok_rows], values[:tok_rows]], axis=1)
    padded = with_halo(keys_values, (("seq", 0),), HALF)
    block = QB
    window_extent = block + 2 * HALF

    def one_block(number):
        start = number * block
        query_matrix = lax.dynamic_slice_in_dim(query, start, block, 0).reshape(
            block, local_heads, HD
        )
        near_rows = lax.dynamic_slice_in_dim(padded, start, window_extent, 0)
        near_keys = near_rows[:, :local_width].reshape(window_extent, local_heads, HD)
        near_values = near_rows[:, local_width:].reshape(window_extent, local_heads, HD)
        near = (
            jnp.einsum("qhd,khd->hqk", query_matrix, near_keys, preferred_element_type=jnp.float32)
            * score_scale
        )
        first = seq_place * tok_rows + start
        qpos = first + jnp.arange(block, dtype=jnp.int32)
        kpos = first - HALF + jnp.arange(window_extent, dtype=jnp.int32)
        valid = (
            (jnp.abs(qpos[:, None] - kpos[None, :]) <= HALF)
            & (kpos >= 0)[None, :]
            & (kpos < total_tokens)[None, :]
        )
        near = jnp.where(valid[None], near, MASKED)
        distant_mask = (
            jnp.einsum(
                "taw,caw->atc", query_matrix, memory_slot_keys, preferred_element_type=jnp.float32
            )
            * score_scale
            - slot_bias[:, None, :]
        )
        scores = jnp.concatenate([near, distant_mask], axis=2)
        top = jnp.max(scores, axis=2, keepdims=True)
        exponent_terms = jnp.exp(scores - top)
        total = jnp.sum(exponent_terms, axis=2)
        attention_probabilities = exponent_terms.astype(jnp.bfloat16)
        numer = jnp.einsum(
            "hqk,khd->qhd",
            attention_probabilities[:, :, :window_extent],
            near_values,
            preferred_element_type=jnp.float32,
        )
        numer = numer + jnp.einsum(
            "lse,elf->slf",
            attention_probabilities[:, :, window_extent:],
            memory_slot_values,
            preferred_element_type=jnp.float32,
        )
        return (
            (numer / jnp.transpose(total)[:, :, None])
            .astype(jnp.bfloat16)
            .reshape(block, local_width)
        )

    token_mix = lax.map(one_block, jnp.arange(tok_rows // block, dtype=jnp.int32)).reshape(
        tok_rows, local_width
    )
    unnormalized_scores = (
        jnp.einsum(
            "gki,pki->kgp", memory_slot_query, token_key_rows, preferred_element_type=jnp.float32
        )
        * score_scale
        - slot_bias[:, :, None]
    )
    local_top = jnp.max(unnormalized_scores, axis=2)
    exponent_terms = jnp.exp(unnormalized_scores - local_top[:, :, None])
    local_sum = jnp.transpose(jnp.sum(exponent_terms, axis=2))
    local_num = jnp.einsum(
        "xzg,gxw->zxw",
        exponent_terms.astype(jnp.bfloat16),
        token_value_rows,
        preferred_element_type=jnp.float32,
    )
    local_top = jnp.transpose(local_top)

    def combine(first_part, second_part):
        top = jnp.maximum(first_part[0], second_part[0])
        weight_first = jnp.exp(first_part[0] - top)
        weight_second = jnp.exp(second_part[0] - top)
        sums = weight_first * first_part[1] + weight_second * second_part[1]
        numers = (
            weight_first[:, :, None] * first_part[2] + weight_second[:, :, None] * second_part[2]
        )
        return (top, sums, numers)

    merged_parts = merged((local_top, local_sum, local_num), "seq", combine)
    own_sum = lax.dynamic_slice_in_dim(merged_parts[1], seq_place * slot_rows, slot_rows, 0)
    own_num = lax.dynamic_slice_in_dim(merged_parts[2], seq_place * slot_rows, slot_rows, 0)
    slot_mix = (own_num / own_sum[:, :, None]).astype(jnp.bfloat16).reshape(slot_rows, local_width)
    mixed = jnp.concatenate([token_mix, slot_mix], axis=0)
    partial_rows = jnp.dot(
        mixed,
        lax.all_gather(w_output, "seq", axis=1, tiled=True),
        preferred_element_type=jnp.float32,
    )
    summed = lax.psum_scatter(
        partial_rows.astype(jnp.bfloat16), "tensor", scatter_dimension=1, tiled=True
    ).astype(jnp.float32)
    residual = jnp.concatenate([state, memory], axis=0).astype(jnp.float32) + summed
    squares = lax.psum(jnp.sum(residual * residual, axis=1), "tensor")
    normed_rows = (residual * lax.rsqrt(squares / D + EPS)[:, None] * norm_gain[None, :]).astype(
        jnp.bfloat16
    )
    new_state = jnp.where((remaining > 0)[:, None], normed_rows[:tok_rows], state)
    new_memory = normed_rows[tok_rows:]
    return (new_state, new_memory)


def solution(mesh):
    placed = (
        P("seq", "tensor"),
        P("seq", "tensor"),
        P("seq", "tensor"),
        P("seq", "tensor"),
        P("seq", "tensor"),
        P("tensor", "seq"),
        P("tensor"),
        P("seq"),
        P(),
    )
    return jax.shard_map(
        shards,
        mesh=mesh,
        in_specs=placed,
        out_specs=(P("seq", "tensor"), P("seq", "tensor")),
        check_vma=False,
    )
```

profile of v0, /device:TPU:1, one launch (start us, length us, event | category | flops | bytes accessed | tf_op | source)
XLA Modules:
  0.0 714.2 jit_solution(8940133622111685820)
XLA Ops:
  10.7 16.0 %all_gather.40 = bf16[16,2048]{1,0:T(8,128)(2,1)S(1)} all-gather(bf16[16,256]{1,0:T(8,128)(2,1)} %param.14), channel_id=1, replica_groups=mesh['seq'=32,'tensor'=8] {'tensor'}, dimensions={1}, use_global_device_ids=true | all-gather | bytes 73728 | tf_op jit(solution)/shard_map/all_gather | solution.py:61
  26.8 25.3 %all-gather.10.cloned.1.call-done = bf16[1024,2048]{1,0:T(8,128)(2,1)} async-done(((bf16[1024,256]{1,0:T(8,128)(2,1)}), bf16[1024,2048]{1,0:T(8,128)(2,1)}) %all-gather.10.cloned.1.call-update) | async-done | bytes 4194320 | tf_op jit(solution)/shard_map/all_gather | solution.py:60
  52.1 4.7 constant_dynamic-update-slice_fusion.2
  57.4 69.1 %all-gather.14.cloned.1.call-done = bf16[2048,256]{1,0:T(8,128)(2,1)} async-done(((bf16[64,256]{1,0:T(8,128)(2,1)}), bf16[2048,256]{1,0:T(8,128)(2,1)}) %all-gather.14.cloned.1.call-update) | async-done | bytes 1048592 | tf_op jit(solution)/shard_map/all_gather | solution.py:67
  126.5 3.8 convolution_convert_fusion.2
  130.4 72.6 %all-gather.12.cloned.1.call-done = bf16[2048,256]{1,0:T(8,128)(2,1)} async-done(((bf16[64,256]{1,0:T(8,128)(2,1)}), bf16[2048,256]{1,0:T(8,128)(2,1)}) %all-gather.12.cloned.1.call-update) | async-done | bytes 1048592 | tf_op jit(solution)/shard_map/all_gather | solution.py:66
  203.0 3.8 convolution_convert_fusion.3
  206.9 72.4 %all-gather.16.cloned.1.call-done = bf16[2048,256]{1,0:T(8,128)(2,1)} async-done(((bf16[64,256]{1,0:T(8,128)(2,1)}), bf16[2048,256]{1,0:T(8,128)(2,1)}) %all-gather.16.cloned.1.call-update) | async-done | bytes 1048592 | tf_op jit(solution)/shard_map/all_gather | solution.py:65
  279.3 3.8 convolution_convert_fusion.1
  284.1 36.9 %all_gather.44 = bf16[512,768]{1,0:T(8,128)(2,1)S(1)} all-gather(bf16[16,768]{1,0:T(8,128)(2,1)S(1)} %pad_maximum_fusion.4), channel_id=1, replica_groups=mesh['seq'=32,'tensor'=8] {'seq'}, dimensions={0}, use_global_device_ids=true | all-gather | bytes 811008 | tf_op jit(solution)/shard_map/all_gather | solution.py:76
  332.0 36.6 %all-gather = f32[16384,2]{0,1:T(2,128)S(1)} all-gather(f32[512,2]{0,1:T(2,128)S(1)} %bitcast.123), channel_id=2, replica_groups=mesh['seq'=32,'tensor'=8] {'seq'}, dimensions={0}, use_global_device_ids=true | all-gather | bytes 135168 | tf_op jit(solution)/shard_map/all_gather | solution.py:30
  371.9 35.7 %all-gather.1 = f32[16384,2]{0,1:T(2,128)S(1)} all-gather(f32[512,2]{0,1:T(2,128)S(1)} %bitcast.126), channel_id=3, replica_groups=mesh['seq'=32,'tensor'=8] {'seq'}, dimensions={0}, use_global_device_ids=true | all-gather | bytes 135168 | tf_op jit(solution)/shard_map/all_gather | solution.py:30
  409.9 22.6 %while.33 = (s32[]{:T(128)}, bf16[2,512,256]{2,1,0:T(8,128)(2,1)}, s32[2]{0:T(128)}, bf16[1536,512]{1,0:T(8,128)(2,1)S(1)}, s32[]{:T(128)}, /*index=5*/bf16[1040...) while((s32[]{:T(128)}, bf16[2,512,256]{2,1,0:T(8,128)(2,1)}, ...), condition=%wide.region_4.5_spmd.clone, body=%wide.region_0.4_spmd.clone.sunk | while | flops 819334656 | bytes 41282024 | solution.py:138
  432.4 48.4 %all-gather.20.cloned.1.call-done = f32[16384,2,128]{0,2,1:T(8,128)} async-done(((f32[512,2,128]{0,2,1:T(8,128)}), f32[16384,2,128]{0,2,1:T(8,128)}) %all-gather.20.cloned.1.call-update) | async-done | bytes 16777232 | tf_op jit(solution)/shard_map/all_gather | solution.py:30
  482.2 25.0 %copy.46 = f32[16384,2,128]{2,1,0:T(2,128)} copy(f32[16384,2,128]{0,2,1:T(8,128)} %all-gather.20.cloned.1.call-done) | data formatting | bytes 33554432 | tf_op jit(solution)/shard_map/while | solution.py:35
  507.1 140.4 %while.32 = (s32[]{:T(128)}, f32[512,2]{0,1:T(2,128)S(1)}, f32[512,2]{0,1:T(2,128)S(1)}, f32[512,2,128]{2,1,0:T(2,128)S(1)}, f32[32,512,2]{1,2,0:T(2,128)S(1)}, ...) while((s32[]{:T(128)}, f32[512,2]{0,1:T(2,128)S(1)}, ...), condition=%wide.region_8.9_spmd, body=%wide.region_7.8_spmd.sunk | while | flops 399365 | bytes 1630351 | solution.py:35
  508.2 3.5 fusion.77
  512.7 3.5 fusion.77
  517.3 3.5 fusion.77
  539.9 3.5 fusion.77
  544.5 3.5 fusion.77
  647.9 4.5 convolution_convert_fusion
  653.1 34.7 %reduce-scatter.2.cloned.1.call-done = bf16[1040,256]{1,0:T(8,128)(2,1)} async-done(((bf16[1040,2048]{1,0:T(8,128)(2,1)}), bf16[1040,256]{1,0:T(8,128)(2,1)}) %reduce-scatter.2.cloned.1.call-update) | async-done | bytes 532496 | tf_op jit(solution)/shard_map/reduce_scatter | solution.py:179
  689.1 15.3 %psum.7 = f32[1040]{0:T(1024)S(1)} all-reduce(f32[1040]{0:T(1024)S(1)} %multiply_reduce_fusion), channel_id=1, replica_groups=mesh['seq'=32,'tensor'=8] {'tensor'}, use_global_device_ids=true, to_apply=%region_11.12 | all-reduce | flops 1040 | bytes 8320 | tf_op jit(solution)/shard_map/psum | solution.py:183
  (257 shorter events, 170.8 us)
Async XLA Ops:
  7.2 44.9 %all-gather.10.cloned.1.call-start = ((), (), s32[]{:S(2)}) async-start(), calls=%async_computation.1 | async-start | bytes 4718592 | tf_op jit(solution)/shard_map/all_gather | solution.py:60
  7.9 118.6 %all-gather.14.cloned.1.call-start = ((), (), s32[]{:S(2)}) async-start(), calls=%async_computation.3 | async-start | bytes 1081344 | tf_op jit(solution)/shard_map/all_gather | solution.py:67
  8.6 194.4 %all-gather.12.cloned.1.call-start = ((), (), s32[]{:S(2)}) async-start(), calls=%async_computation.2 | async-start | bytes 1081344 | tf_op jit(solution)/shard_map/all_gather | solution.py:66
  9.4 270.0 %all-gather.16.cloned.1.call-start = ((), (), s32[]{:S(2)}) async-start(), calls=%async_computation.4 | async-start | bytes 1081344 | tf_op jit(solution)/shard_map/all_gather | solution.py:65
  10.0 470.9 %all-gather.20.cloned.1.call-start = ((), (), s32[]{:S(2)}) async-start(), calls=%async_computation.7 | async-start | bytes 17301504 | tf_op jit(solution)/shard_map/all_gather | solution.py:30
  10.7 46.1 %copy-start.11 = (f32[512]{0:T(512)}, f32[512]{0:T(512)S(1)}, u32[]{:S(2)}) copy-start(f32[512]{0:T(512)S(1)} %subtract_abs_fusion) | copy-start | bytes 6148
  26.7 30.1 %copy-start.14 = (f32[2]{0:T(128)}, f32[2]{0:T(128)S(1)}, u32[]{:S(2)}) copy-start(f32[2]{0:T(128)S(1)} %power_multiply_fusion) | copy-start | bytes 28
  26.8 295.1 %copy-start.13 = (f32[2,512]{1,0:T(2,128)}, f32[2,512]{1,0:T(2,128)S(1)}, u32[]{:S(2)}) copy-start(f32[2,512]{1,0:T(2,128)S(1)} %broadcast_multiply_fusion.1) | copy-start | bytes 12292
  284.1 39.7 %copy-start.8 = (bf16[1024,256]{0,1:T(8,128)(2,1)S(1)}, bf16[1024,256]{0,1:T(8,128)(2,1)}, u32[]{:S(2)}) copy-start(bf16[1024,256]{0,1:T(8,128)(2,1)} %copy.45) | copy-start | bytes 1572868
  321.9 1.9 copy-start
  325.9 322.0 %all-gather.18.cloned.1.call-start = ((), (), s32[]{:S(2)}) async-start(), calls=%async_computation.5 | async-start | bytes 1081344 | tf_op jit(solution)/shard_map/all_gather | solution.py:176
  326.5 361.3 %reduce-scatter.2.cloned.1.call-start = ((), (), s32[]{:S(2)}) async-start(), calls=%async_computation.6 | async-start | bytes 4792320 | tf_op jit(solution)/shard_map/reduce_scatter | solution.py:179
  326.6 81.1 %collective-permute-start = (bf16[256,512]{1,0:T(8,128)(2,1)S(1)}, bf16[256,512]{1,0:T(8,128)(2,1)S(1)}, u32[]{:S(2)}, u32[]{:S(2)}) collective-permute-start(bf16[256,512]{1,0:T(8,128)(2,1)S(1)} %get-tuple-element.403), channel_id=1, source_target_pairs={{0,8},{8,16},{16,24},{24,32},{32,40},{40,48},{48,56},{56,64},{64,7... | collective-permute-start | bytes 786440 | tf_op jit(solution)/shard_map/ppermute | solution.py:23
  329.1 79.2 %collective-permute-start.1 = (bf16[256,512]{1,0:T(8,128)(2,1)S(1)}, bf16[256,512]{1,0:T(8,128)(2,1)}, u32[]{:S(2)}, u32[]{:S(2)}) collective-permute-start(bf16[256,512]{1,0:T(8,128)(2,1)S(1)} %get-tuple-element.404), channel_id=1, source_target_pairs={{8,0},{16,8},{24,16},{32,24},{40,32},{48,40},{56,48},{64,56},{72,6... | collective-permute-start | bytes 786440 | tf_op jit(solution)/shard_map/ppermute | solution.py:24
  409.9 2.9 copy-start.3
  417.6 2.1 copy-start.9
  418.8 2.3 copy-start.4
  421.1 2.9 copy-start.3
  428.8 2.1 copy-start.9
  430.1 2.3 copy-start.4
  507.1 140.7 %copy-start.7 = (bf16[2,512,256]{2,1,0:T(8,128)(2,1)S(1)}, bf16[2,512,256]{2,1,0:T(8,128)(2,1)}, u32[]{:S(2)}) copy-start(bf16[2,512,256]{2,1,0:T(8,128)(2,1)} %get-tuple-element.294) | copy-start | bytes 1572868
  652.4 35.4 %copy-start.2 = (bf16[1024,256]{1,0:T(8,128)(2,1)S(1)}, bf16[1024,256]{1,0:T(8,128)(2,1)}, u32[]{:S(2)}) copy-start(bf16[1024,256]{1,0:T(8,128)(2,1)} %param.13) | copy-start | bytes 1572868
  652.4 35.4 %copy-start.12 = (bf16[16,256]{1,0:T(8,128)(2,1)S(1)}, bf16[16,256]{1,0:T(8,128)(2,1)}, u32[]{:S(2)}) copy-start(bf16[16,256]{1,0:T(8,128)(2,1)} %param.14) | copy-start | bytes 24580
  652.4 52.0 %copy-start.16 = (f32[256]{0:T(256)S(1)}, f32[256]{0:T(256)}, u32[]{:S(2)}) copy-start(f32[256]{0:T(256)} %param.19) | copy-start | bytes 3076
  (8 other events, 8.5 us)
Sparse Core Ops, SparseCore 0:
  9.8 42.2 all-gather.9
  54.7 71.8 all-gather.13
  129.1 73.8 all-gather.11
  205.5 73.8 all-gather.15
  326.0 154.7 all-gather.19
  483.3 68.5 all-gather.17
  652.5 35.1 reduce-scatter.1
where the time goes:
time: 718 us; the launch traced here: 714 us
  waiting for transfers between devices  326 us (45%)
  other arithmetic  144 us (20%)
  blocking collectives  141 us (20%)
  local copies, waits for them, and re-layouts  55.6 us (8%)
  matrix products  26.7 us (4%)
  between operations  14.4 us (2%)
    add x31, other arithmetic, combine(): weight_first[:, :, None] * first_part[2]  108 us
    all_gather x1, waiting for transfers between devices, shards(): lax.all_gather(w_key, 'seq', axis=0, tiled=True)  72.6 us
    all_gather x1, waiting for transfers between devices, shards(): lax.all_gather(w_query, 'seq', axis=0, tiled=True)  72.4 us
    all_gather x2, blocking collectives, merged(): gathered = jax.tree.map(lambda a: lax.all_gather(a, axis), part)  72.3 us
    all_gather x1, waiting for transfers between devices, shards(): lax.all_gather(w_value, 'seq', axis=0, tiled=True)  69.1 us
    all_gather x1, waiting for transfers between devices, merged(): gathered = jax.tree.map(lambda a: lax.all_gather(a, axis), part)  48.4 us
    all_gather x1, blocking collectives, shards(): all_slots = lax.all_gather(slot_heads, 'seq', axis=0, tiled=True)  36.9 us
    reduce_scatter x1, waiting for transfers between devices, shards(): lax.psum_scatter(partial_rows.astype(jnp.bfloat16), 'tensor', scatter_dim...  34.7 us
  transfers between devices with their start and end apart: 9, of which 6 were waited for; matrix products, arithmetic and copies ran while one was open for 29% of the time, Pallas kernels for 0%

commit v1 on v0

--- a/solution.py
+++ b/solution.py
@@ -11,6 +11,12 @@
 QB = 512
 EPS = 1e-05
 MASKED = -1e30
+
+
+def gather_from_all(x, axis, dim):
+    size = lax.axis_size(axis)
+    repeats = [size if d == dim else 1 for d in range(x.ndim)]
+    return lax.all_to_all(jnp.tile(x, repeats), axis, split_axis=dim, concat_axis=dim, tiled=True)
 
 
 def with_halo(array, sides, width):
@@ -64,7 +70,7 @@
     pieces = (
         lax.all_gather(w_query, "seq", axis=0, tiled=True),
         lax.all_gather(w_key, "seq", axis=0, tiled=True),
-        lax.all_gather(w_value, "seq", axis=0, tiled=True),
+        gather_from_all(w_value, "seq", 0),
     )
     query_acc, key_acc, value_acc = tuple(
         (jnp.dot(rows_full, piece, preferred_element_type=jnp.float32) for piece in pieces)

time: 718 us -> 642 us (0.89)
  waiting for transfers between devices: 326 us -> 238 us
  starting transfers between devices: 4.04 us -> 16 us
    all_gather x1 -> x0, waiting for transfers between devices: 69.1 us -> none  [shards(): lax.all_gather(w_value, 'seq', axis=0, tiled=True)]
    all_to_all x0 -> x1, starting transfers between devices: none -> 12 us  [gather_from_all(): lax.all_to_all(jnp.tile(x, repeats), axis, split_axis=dim, concat_axis=di...]
    all_gather x1, waiting for transfers between devices: 25.3 us -> 13.9 us  [shards(): lax.all_gather(state, 'tensor', axis=1, tiled=True)]
  transfers between devices with their start and end apart: 9 -> 9, of which waited for: 6 -> 5; matrix products, arithmetic and copies ran while one was open for 29% -> 32% of each run, Pallas kernels for 0% -> 0%
where the time goes in v1:
time: 642 us; the launch traced here: 638 us
  waiting for transfers between devices  238 us (37%)
  other arithmetic  144 us (22%)
  blocking collectives  139 us (22%)
  local copies, waits for them, and re-layouts  57.6 us (9%)
  matrix products  26.4 us (4%)
  starting transfers between devices  16 us (2%)
  between operations  14.4 us (2%)
    add x31, other arithmetic, combine(): weight_first[:, :, None] * first_part[2]  108 us
    all_gather x1, waiting for transfers between devices, shards(): lax.all_gather(w_query, 'seq', axis=0, tiled=True)  72.5 us
    all_gather x2, blocking collectives, merged(): gathered = jax.tree.map(lambda a: lax.all_gather(a, axis), part)  72.4 us
    all_gather x1, waiting for transfers between devices, shards(): lax.all_gather(w_key, 'seq', axis=0, tiled=True)  65.6 us
    all_gather x1, waiting for transfers between devices, merged(): gathered = jax.tree.map(lambda a: lax.all_gather(a, axis), part)  48.2 us
    all_gather x1, blocking collectives, shards(): all_slots = lax.all_gather(slot_heads, 'seq', axis=0, tiled=True)  36.9 us
    reduce_scatter x1, waiting for transfers between devices, shards(): lax.psum_scatter(partial_rows.astype(jnp.bfloat16), 'tensor', scatter_dim...  34.6 us
    while x2, local copies, waits for them, and re-layouts, merged(): lax.fori_loop(1, lax.axis_size(axis), lambda source, state: combine(state...  25.2 us
  transfers between devices with their start and end apart: 9, of which 5 were waited for; matrix products, arithmetic and copies ran while one was open for 32% of the time, Pallas kernels for 0%

profile of v1, /device:TPU:1, one launch (start us, length us, event | category | flops | bytes accessed | tf_op | source)
XLA Modules:
  0.0 637.9 jit_solution(959577427608948657)
XLA Ops:
  10.5 12.0 %all-to-all-start = ((bf16[32,64,256]{2,1,0:T(8,128)(2,1)}), bf16[32,64,256]{2,1,0:T(8,128)(2,1)S(1)}, u32[]{:S(2)}, u32[]{:S(2)}) async-start(bf16[32,64,256]{2,1,0:T(8,128)(2,1)} %tile.2), calls=%async_computation | async-start | bytes 2097152 | tf_op jit(solution)/shard_map/all_to_all | solution.py:19
  24.0 14.2 %all_gather.37 = bf16[16,2048]{1,0:T(8,128)(2,1)S(1)} all-gather(bf16[16,256]{1,0:T(8,128)(2,1)} %param.14), channel_id=1, replica_groups=mesh['seq'=32,'tensor'=8] {'tensor'}, dimensions={1}, use_global_device_ids=true | all-gather | bytes 73728 | tf_op jit(solution)/shard_map/all_gather | solution.py:67
  38.3 13.9 %all-gather.9.cloned.1.call-done = bf16[1024,2048]{1,0:T(8,128)(2,1)} async-done(((bf16[1024,256]{1,0:T(8,128)(2,1)}), bf16[1024,2048]{1,0:T(8,128)(2,1)}) %all-gather.9.cloned.1.call-update) | async-done | bytes 4194320 | tf_op jit(solution)/shard_map/all_gather | solution.py:66
  52.3 4.7 constant_dynamic-update-slice_fusion.2
  61.2 65.6 %all-gather.11.cloned.1.call-done = bf16[2048,256]{1,0:T(8,128)(2,1)} async-done(((bf16[64,256]{1,0:T(8,128)(2,1)}), bf16[2048,256]{1,0:T(8,128)(2,1)}) %all-gather.11.cloned.1.call-update) | async-done | bytes 1048592 | tf_op jit(solution)/shard_map/all_gather | solution.py:72
  126.7 3.8 convolution_convert_fusion.3
  130.6 72.5 %all-gather.13.cloned.1.call-done = bf16[2048,256]{1,0:T(8,128)(2,1)} async-done(((bf16[64,256]{1,0:T(8,128)(2,1)}), bf16[2048,256]{1,0:T(8,128)(2,1)}) %all-gather.13.cloned.1.call-update) | async-done | bytes 1048592 | tf_op jit(solution)/shard_map/all_gather | solution.py:71
  203.2 3.8 convolution_convert_fusion.1
  208.0 36.9 %all_gather.40 = bf16[512,768]{1,0:T(8,128)(2,1)S(1)} all-gather(bf16[16,768]{1,0:T(8,128)(2,1)S(1)} %pad_maximum_fusion.4), channel_id=1, replica_groups=mesh['seq'=32,'tensor'=8] {'seq'}, dimensions={0}, use_global_device_ids=true | all-gather | bytes 811008 | tf_op jit(solution)/shard_map/all_gather | solution.py:82
  255.8 36.7 %all-gather = f32[16384,2]{0,1:T(2,128)S(1)} all-gather(f32[512,2]{0,1:T(2,128)S(1)} %bitcast.125), channel_id=2, replica_groups=mesh['seq'=32,'tensor'=8] {'seq'}, dimensions={0}, use_global_device_ids=true | all-gather | bytes 135168 | tf_op jit(solution)/shard_map/all_gather | solution.py:36
  295.8 35.7 %all-gather.1 = f32[16384,2]{0,1:T(2,128)S(1)} all-gather(f32[512,2]{0,1:T(2,128)S(1)} %bitcast.128), channel_id=3, replica_groups=mesh['seq'=32,'tensor'=8] {'seq'}, dimensions={0}, use_global_device_ids=true | all-gather | bytes 135168 | tf_op jit(solution)/shard_map/all_gather | solution.py:36
  333.7 22.7 %while.33 = (s32[]{:T(128)}, bf16[2,512,256]{2,1,0:T(8,128)(2,1)}, s32[2]{0:T(128)}, bf16[1536,512]{1,0:T(8,128)(2,1)S(1)}, s32[]{:T(128)}, /*index=5*/bf16[1040...) while((s32[]{:T(128)}, bf16[2,512,256]{2,1,0:T(8,128)(2,1)}, ...), condition=%wide.region_4.5_spmd.clone, body=%wide.region_0.4_spmd.clone.sunk | while | flops 819334656 | bytes 41282024 | solution.py:144
  356.4 48.2 %all-gather.17.cloned.1.call-done = f32[16384,2,128]{0,2,1:T(8,128)} async-done(((f32[512,2,128]{0,2,1:T(8,128)}), f32[16384,2,128]{0,2,1:T(8,128)}) %all-gather.17.cloned.1.call-update) | async-done | bytes 16777232 | tf_op jit(solution)/shard_map/all_gather | solution.py:36
  406.0 25.0 %copy.46 = f32[16384,2,128]{2,1,0:T(2,128)} copy(f32[16384,2,128]{0,2,1:T(8,128)} %all-gather.17.cloned.1.call-done) | data formatting | bytes 33554432 | tf_op jit(solution)/shard_map/while | solution.py:41
  430.9 140.4 %while.32 = (s32[]{:T(128)}, f32[512,2]{0,1:T(2,128)S(1)}, f32[512,2]{0,1:T(2,128)S(1)}, f32[512,2,128]{2,1,0:T(2,128)S(1)}, f32[32,512,2]{1,2,0:T(2,128)S(1)}, ...) while((s32[]{:T(128)}, f32[512,2]{0,1:T(2,128)S(1)}, ...), condition=%wide.region_8.9_spmd, body=%wide.region_7.8_spmd.sunk | while | flops 399365 | bytes 1630351 | solution.py:41
  432.0 3.5 fusion.77
  436.5 3.5 fusion.77
  441.1 3.5 fusion.77
  445.6 3.5 fusion.77
  463.7 3.5 fusion.77
  468.2 3.5 fusion.77
  571.7 4.5 convolution_convert_fusion
  576.9 34.6 %reduce-scatter.2.cloned.1.call-done = bf16[1040,256]{1,0:T(8,128)(2,1)} async-done(((bf16[1040,2048]{1,0:T(8,128)(2,1)}), bf16[1040,256]{1,0:T(8,128)(2,1)}) %reduce-scatter.2.cloned.1.call-update) | async-done | bytes 532496 | tf_op jit(solution)/shard_map/reduce_scatter | solution.py:185
  612.8 15.4 %psum.7 = f32[1040]{0:T(1024)S(1)} all-reduce(f32[1040]{0:T(1024)S(1)} %multiply_reduce_fusion), channel_id=1, replica_groups=mesh['seq'=32,'tensor'=8] {'tensor'}, use_global_device_ids=true, to_apply=%region_11.12 | all-reduce | flops 1040 | bytes 8320 | tf_op jit(solution)/shard_map/psum | solution.py:189
  (257 shorter events, 172.2 us)
Async XLA Ops:
  7.2 45.1 %all-gather.9.cloned.1.call-start = ((), (), s32[]{:S(2)}) async-start(), calls=%async_computation.2 | async-start | bytes 4718592 | tf_op jit(solution)/shard_map/all_gather | solution.py:66
  7.9 118.8 %all-gather.11.cloned.1.call-start = ((), (), s32[]{:S(2)}) async-start(), calls=%async_computation.3 | async-start | bytes 1081344 | tf_op jit(solution)/shard_map/all_gather | solution.py:72
  10.5 47.1 %all-to-all-start = ((bf16[32,64,256]{2,1,0:T(8,128)(2,1)}), bf16[32,64,256]{2,1,0:T(8,128)(2,1)S(1)}, u32[]{:S(2)}, u32[]{:S(2)}) async-start(bf16[32,64,256]{2,1,0:T(8,128)(2,1)} %tile.2), calls=%async_computation | async-start | bytes 2097152 | tf_op jit(solution)/shard_map/all_to_all | solution.py:19
  22.5 180.7 %all-gather.13.cloned.1.call-start = ((), (), s32[]{:S(2)}) async-start(), calls=%async_computation.4 | async-start | bytes 1081344 | tf_op jit(solution)/shard_map/all_gather | solution.py:71
  23.3 381.4 %all-gather.17.cloned.1.call-start = ((), (), s32[]{:S(2)}) async-start(), calls=%async_computation.7 | async-start | bytes 17301504 | tf_op jit(solution)/shard_map/all_gather | solution.py:36
  24.0 33.0 %copy-start.11 = (f32[512]{0:T(512)}, f32[512]{0:T(512)S(1)}, u32[]{:S(2)}) copy-start(f32[512]{0:T(512)S(1)} %subtract_abs_fusion) | copy-start | bytes 6148
  38.3 18.7 %copy-start.14 = (f32[2]{0:T(128)}, f32[2]{0:T(128)S(1)}, u32[]{:S(2)}) copy-start(f32[2]{0:T(128)S(1)} %power_multiply_fusion) | copy-start | bytes 28
  38.3 207.4 %copy-start.13 = (f32[2,512]{1,0:T(2,128)}, f32[2,512]{1,0:T(2,128)S(1)}, u32[]{:S(2)}) copy-start(f32[2,512]{1,0:T(2,128)S(1)} %broadcast_multiply_fusion.1) | copy-start | bytes 12292
  208.0 39.7 %copy-start.8 = (bf16[1024,256]{0,1:T(8,128)(2,1)S(1)}, bf16[1024,256]{0,1:T(8,128)(2,1)}, u32[]{:S(2)}) copy-start(bf16[1024,256]{0,1:T(8,128)(2,1)} %copy.45) | copy-start | bytes 1572868
  245.8 2.0 copy-start
  249.8 321.9 %all-gather.15.cloned.1.call-start = ((), (), s32[]{:S(2)}) async-start(), calls=%async_computation.5 | async-start | bytes 1081344 | tf_op jit(solution)/shard_map/all_gather | solution.py:182
  250.4 361.1 %reduce-scatter.2.cloned.1.call-start = ((), (), s32[]{:S(2)}) async-start(), calls=%async_computation.6 | async-start | bytes 4792320 | tf_op jit(solution)/shard_map/reduce_scatter | solution.py:185
  250.5 81.0 %collective-permute-start = (bf16[256,512]{1,0:T(8,128)(2,1)S(1)}, bf16[256,512]{1,0:T(8,128)(2,1)S(1)}, u32[]{:S(2)}, u32[]{:S(2)}) collective-permute-start(bf16[256,512]{1,0:T(8,128)(2,1)S(1)} %get-tuple-element.403), channel_id=1, source_target_pairs={{0,8},{8,16},{16,24},{24,32},{32,40},{40,48},{48,56},{56,64},{64,7... | collective-permute-start | bytes 786440 | tf_op jit(solution)/shard_map/ppermute | solution.py:29
  252.9 79.2 %collective-permute-start.1 = (bf16[256,512]{1,0:T(8,128)(2,1)S(1)}, bf16[256,512]{1,0:T(8,128)(2,1)}, u32[]{:S(2)}, u32[]{:S(2)}) collective-permute-start(bf16[256,512]{1,0:T(8,128)(2,1)S(1)} %get-tuple-element.404), channel_id=1, source_target_pairs={{8,0},{16,8},{24,16},{32,24},{40,32},{48,40},{56,48},{64,56},{72,6... | collective-permute-start | bytes 786440 | tf_op jit(solution)/shard_map/ppermute | solution.py:30
  333.7 2.9 copy-start.3
  341.5 2.1 copy-start.9
  342.7 2.3 copy-start.4
  345.1 2.9 copy-start.3
  352.8 2.1 copy-start.9
  354.1 2.3 copy-start.4
  430.9 140.7 %copy-start.7 = (bf16[2,512,256]{2,1,0:T(8,128)(2,1)S(1)}, bf16[2,512,256]{2,1,0:T(8,128)(2,1)}, u32[]{:S(2)}) copy-start(bf16[2,512,256]{2,1,0:T(8,128)(2,1)} %get-tuple-element.294) | copy-start | bytes 1572868
  576.2 35.3 %copy-start.2 = (bf16[1024,256]{1,0:T(8,128)(2,1)S(1)}, bf16[1024,256]{1,0:T(8,128)(2,1)}, u32[]{:S(2)}) copy-start(bf16[1024,256]{1,0:T(8,128)(2,1)} %param.13) | copy-start | bytes 1572868
  576.2 35.3 %copy-start.12 = (bf16[16,256]{1,0:T(8,128)(2,1)S(1)}, bf16[16,256]{1,0:T(8,128)(2,1)}, u32[]{:S(2)}) copy-start(bf16[16,256]{1,0:T(8,128)(2,1)} %param.14) | copy-start | bytes 24580
  576.2 52.0 %copy-start.16 = (f32[256]{0:T(256)S(1)}, f32[256]{0:T(256)}, u32[]{:S(2)}) copy-start(f32[256]{0:T(256)} %param.19) | copy-start | bytes 3076
  (8 other events, 8.5 us)
Sparse Core Ops, SparseCore 0:
  9.8 42.4 all-gather.8
  54.8 71.8 all-gather.10
  129.3 73.8 all-gather.12
  249.9 154.7 all-gather.16
  407.1 68.5 all-gather.14
  576.4 35.1 reduce-scatter.1
